TPU v7x, 256 devices: a whole 4x4x8 slice. The times are simulated.
256 devices in a mesh: dp: 8 (over x, core), group: 32 (over z, y).
Axes of the slice: x: 4, y: 4, z: 8, core: 2. Of those that a mesh axis runs over, the one named last changes fastest.
Arguments:
- embeds: bfloat16 [65536, 1024], P(('dp', 'group')), may hold values from -6 to 6
- row_ids: int32 [65536], P(('dp', 'group')), may hold values from 0 to 63
- neighbors: int32 [256, 3], P('dp'), may hold values from 0 to 31, as said below
- w_first: bfloat16 [1024, 4096], P(None, 'dp'), may hold values from -0.1875 to 0.1875
- w_second: bfloat16 [4096, 1024], P('dp'), may hold values from -0.09375 to 0.09375
Outputs:
- grad_first: float32 [1024, 4096], P('group', 'dp')
- grad_second: float32 [4096, 1024], P('dp', 'group')
- grad_unit: float32 [65536, 1024], P(('dp', 'group'))
Inputs may be any that keep to these rules, and one draw needn't show every extreme that they name: `neighbors`: within a row the 3 entries differ from one another and from the row's own index b % 32.
All inputs are finite; a program needn't handle non-finite values.
Results may differ from a plain program's by a relative error of at most 0.013.
Values may be sent and summed in bfloat16 or wider, within the bound.
No kernel may reach another device: no remote copies, remote signals or barrier semaphores. Data moves between devices by JAX's collectives and lax.ppermute only.
A program may use at most 64 MiB of HBM per device.

v0:
```python
import jax
import jax.numpy as jnp
from jax import lax
from jax.sharding import PartitionSpec as P

EPS = 1e-06
TEMP = 10.0
SHIFT = -5.0


def gelu_fwd(value):
    return jax.nn.gelu(value, approximate=True)


def gelu_back(pre, grad):
    _, back = jax.vjp(gelu_fwd, pre)
    return back(grad)[0]


def per_device(embeds, row_ids, neighbors, w_first, w_second):
    owners = lax.axis_size("group")
    block = embeds.shape[0]
    piece = block // owners
    width = w_second.shape[1]
    listed = neighbors.shape[1]
    gathered = lax.all_gather(embeds, "dp", axis=0, tiled=True)
    pre = jnp.dot(gathered, w_first, preferred_element_type=jnp.float32)
    hidden = gelu_fwd(pre).astype(jnp.bfloat16)
    proj = lax.psum_scatter(
        jnp.dot(hidden, w_second, preferred_element_type=jnp.float32).astype(jnp.bfloat16),
        "dp",
        scatter_dimension=0,
        tiled=True,
    ).astype(jnp.float32)
    inv = lax.rsqrt(jnp.mean(proj * proj, axis=-1, keepdims=True) + EPS)
    unit = proj * inv
    unit_b = unit.astype(jnp.bfloat16)
    held, held_ids = (
        lax.all_to_all(
            unit_b.reshape(owners, piece, width), "group", split_axis=0, concat_axis=0, tiled=True
        ),
        lax.all_to_all(
            row_ids.reshape(owners, piece), "group", split_axis=0, concat_axis=0, tiled=True
        ),
    )
    order = neighbors.T
    outgoing = jnp.take(held, order, axis=0)
    outgoing_ids = jnp.take(held_ids, order, axis=0)
    fetched, fetched_ids = (
        lax.all_to_all(outgoing, "group", split_axis=1, concat_axis=1, tiled=True),
        lax.all_to_all(outgoing_ids, "group", split_axis=1, concat_axis=1, tiled=True),
    )
    cand = jnp.concatenate([unit_b[None], fetched.reshape(listed, block, width)], 0)
    cand_ids = jnp.concatenate([row_ids[None], fetched_ids.reshape(listed, block)], 0)
    logits = (
        TEMP / width * jnp.einsum("rp,kcp->krc", unit_b, cand, preferred_element_type=jnp.float32)
        + SHIFT
    )
    sign = jnp.where(row_ids[None, :, None] == cand_ids[:, None, :], 1.0, -1.0).astype(jnp.float32)
    weight = (-sign * jax.nn.sigmoid(-sign * logits) * (TEMP / width)).astype(jnp.bfloat16)
    grad_own = jnp.einsum("krc,kcp->rp", weight, cand, preferred_element_type=jnp.float32)
    grad_cand = jnp.einsum("krc,rp->kcp", weight, unit_b, preferred_element_type=jnp.float32)
    returned = lax.all_to_all(
        grad_cand[1:].reshape(listed, owners, piece, width),
        "group",
        split_axis=1,
        concat_axis=1,
        tiled=True,
    )
    select = (order[:, :, None] == jnp.arange(owners, dtype=jnp.int32)[None, None, :]).astype(
        jnp.float32
    )
    summed = jnp.einsum("krb,krqp->bqp", select, returned, precision=lax.Precision.HIGHEST)
    collected = lax.all_to_all(summed, "group", split_axis=0, concat_axis=0, tiled=True)
    grad_unit = grad_own + grad_cand[0] + collected.reshape(block, width)
    grad_proj = inv * (grad_unit - unit * jnp.mean(unit * grad_unit, axis=-1, keepdims=True))
    grad_all = lax.all_gather(grad_proj.astype(jnp.bfloat16), "dp", axis=0, tiled=True)
    second_local = lax.dot_general(
        hidden, grad_all, (((0,), (0,)), ((), ())), preferred_element_type=jnp.float32
    )
    grad_hidden = lax.dot_general(
        grad_all, w_second, (((1,), (1,)), ((), ())), preferred_element_type=jnp.float32
    )
    grad_pre = gelu_back(pre, grad_hidden).astype(jnp.bfloat16)
    first_local = lax.dot_general(
        gathered, grad_pre, (((0,), (0,)), ((), ())), preferred_element_type=jnp.float32
    )
    first_out, second_out = (
        lax.psum_scatter(first_local, "group", scatter_dimension=0, tiled=True),
        lax.psum_scatter(second_local, "group", scatter_dimension=1, tiled=True),
    )
    return (first_out, second_out, grad_unit)


def solution(mesh):
    in_specs = (
        P(("dp", "group"), None),
        P(("dp", "group")),
        P("dp", None),
        P(None, "dp"),
        P("dp", None),
    )
    out_specs = (P("group", "dp"), P("dp", "group"), P(("dp", "group"), None))
    return jax.shard_map(
        per_device, mesh=mesh, in_specs=in_specs, out_specs=out_specs, check_vma=False
    )
```

profile of v0, /device:TPU:4, one launch (start us, length us, event | category | flops | bytes accessed | tf_op | source)
XLA Modules:
  0.0 792.0 jit_solution(12244141082356973376)
XLA Ops:
  8.0 38.2 %all-gather.3.cloned.1.call-done = bf16[2048,1024]{1,0:T(8,128)(2,1)} async-done(((bf16[256,1024]{1,0:T(8,128)(2,1)}), bf16[2048,1024]{1,0:T(8,128)(2,1)}) %all-gather.3.cloned.1.call-update) | async-done | bytes 4194320 | tf_op jit(solution)/shard_map/all_gather | solution.py:26
  46.2 4.8 fusion.58
  51.0 2.0 copy-done.6
  53.0 4.8 convolution_convert_fusion
  59.1 9.9 %all-to-all-start = ((s32[32,1,8]{2,1,0:T(1,128)}), s32[32,1,8]{2,1,0:T(1,128)S(1)}, u32[]{:S(2)}, u32[]{:S(2)}) async-start(s32[32,1,8]{2,1,0:T(1,128)} %bitcast.2), calls=%async_computation.1 | async-start | bytes 32768 | tf_op jit(solution)/shard_map/all_to_all | solution.py:42
  69.0 26.2 %reduce-scatter.6.cloned.1.call-done = bf16[256,1024]{1,0:T(8,128)(2,1)} async-done(((bf16[2048,1024]{1,0:T(8,128)(2,1)}), bf16[256,1024]{1,0:T(8,128)(2,1)}) %reduce-scatter.6.cloned.1.call-update) | async-done | bytes 524304 | tf_op jit(solution)/shard_map/reduce_scatter | solution.py:29
  96.4 2.2 fusion.54
  98.6 9.6 %all-to-all-start.2 = ((bf16[32,8,1024]{2,1,0:T(8,128)(2,1)}), bf16[32,8,1024]{2,1,0:T(8,128)(2,1)S(1)}, u32[]{:S(2)}, u32[]{:S(2)}) async-start(bf16[32,8,1024]{2,1,0:T(8,128)(2,1)} %get-tuple-element.19), calls=%async_computation.3 | async-start | bytes 1048576 | tf_op jit(solution)/shard_map/all_to_all | solution.py:39
  109.8 16.9 %all-to-all-done.2 = bf16[32,8,1024]{2,1,0:T(8,128)(2,1)S(1)} async-done(((bf16[32,8,1024]{2,1,0:T(8,128)(2,1)}), bf16[32,8,1024]{2,1,0:T(8,128)(2,1)S(1)}, u32[]{:S(2)}, u32[]{:S(2)}) %all-to-all-start.2) | async-done | bytes 524320 | tf_op jit(solution)/shard_map/all_to_all | solution.py:39
  126.8 4.7 all-to-all-start.1
  132.4 1.3 copy.46
  133.8 7.7 all-to-all-done.1
  141.5 4.0 all-to-all-start.3
  145.6 37.7 %all-to-all-done.3 = bf16[3,32,8,1024]{3,2,0,1:T(8,128)(2,1)S(1)} async-done(((bf16[3,32,8,1024]{3,2,0,1:T(8,128)(2,1)}), bf16[3,32,8,1024]{3,2,0,1:T(8,128)(2,1)S(1)}, u32[]{:S(2)}, u32[]{:S(2)}) %all-to-all-start.3) | async-done | bytes 1572896 | tf_op jit(solution)/shard_map/all_to_all | solution.py:50
  183.5 2.1 fusion.31
  187.2 75.9 %all_to_all.37 = f32[3,32,8,1024]{3,2,0,1:T(8,128)S(1)} all-to-all(f32[3,32,8,1024]{3,2,0,1:T(8,128)S(1)} %copy.50), channel_id=1, replica_groups=mesh['dp'=8,'group'=32] {'group'}, dimensions={1} | all-to-all | bytes 6291456 | tf_op jit(solution)/shard_map/all_to_all | solution.py:63
  263.2 3.1 fusion.14
  266.9 31.0 %all_to_all.38 = f32[32,8,1024]{2,1,0:T(8,128)S(1)} all-to-all(f32[32,8,1024]{2,1,0:T(8,128)S(1)} %copy.52), channel_id=1, replica_groups=mesh['dp'=8,'group'=32] {'group'}, dimensions={0} | all-to-all | bytes 2097152 | tf_op jit(solution)/shard_map/all_to_all | solution.py:74
  300.9 33.7 %all-gather.5.cloned.1.call-done = bf16[2048,1024]{1,0:T(8,128)(2,1)} async-done(((bf16[256,1024]{1,0:T(8,128)(2,1)}), bf16[2048,1024]{1,0:T(8,128)(2,1)}) %all-gather.5.cloned.1.call-update) | async-done | bytes 4194320 | tf_op jit(solution)/shard_map/all_gather | solution.py:77
  334.6 11.6 %fusion.11 = f32[1024,512]{0,1:T(8,128)S(1)} fusion(bf16[2048,1024]{1,0:T(8,128)(2,1)} %all-gather.3.cloned.1.call-done, f32[2048,512]{1,0:T(8,128)} %copy-done.6, bf16[2048,1024]{1,0:T(8,128)(2,1)} %all-gather.5.cloned.1.call-done, bf16[512,1024]{1,0:T(8,128)(2,1)S(1)} %copy-done), kind=kOutput, calls=%fused_computation.18 | convolution fusion | flops 4315938816 | bytes 15728640 | tf_op jit(solution)/shard_map/dot_general | solution.py:85
  346.2 1.9 copy.56
  348.1 7.3 fusion.55
  355.5 210.5 %reduce-scatter.10.cloned.1.call-done = f32[32,512]{1,0:T(8,128)} async-done(((f32[1024,512]{1,0:T(8,128)}), f32[32,512]{1,0:T(8,128)}) %reduce-scatter.10.cloned.1.call-update) | async-done | bytes 65552
  566.0 219.4 %reduce-scatter.8.cloned.1.call-done = f32[512,32]{0,1:T(8,128)} async-done(((f32[512,1024]{0,1:T(8,128)}), f32[512,32]{0,1:T(8,128)}) %reduce-scatter.8.cloned.1.call-update) | async-done | bytes 65552 | tf_op jit(solution)/shard_map/reduce_scatter | solution.py:90
  (47 shorter events, 11.5 us)
Async XLA Ops:
  7.2 45.8 %copy-start = (bf16[512,1024]{1,0:T(8,128)(2,1)S(1)}, bf16[512,1024]{1,0:T(8,128)(2,1)}, u32[]{:S(2)}) copy-start(bf16[512,1024]{1,0:T(8,128)(2,1)} %param.9) | copy-start | bytes 3145732
  7.2 39.0 %all-gather.3.cloned.1.call-start = ((), (), s32[]{:S(2)}) async-start(), calls=%async_computation.9 | async-start | bytes 4718592 | tf_op jit(solution)/shard_map/all_gather | solution.py:26
  7.9 87.3 %reduce-scatter.6.cloned.1.call-start = ((), (), s32[]{:S(2)}) async-start(), calls=%async_computation.10 | async-start | bytes 4718592 | tf_op jit(solution)/shard_map/reduce_scatter | solution.py:29
  51.0 2.0 copy-start.6
  57.8 0.7 copy-start.5
  57.8 50.5 %copy-start.4 = (s32[32,3]{0,1:T(4,128)S(1)}, s32[32,3]{0,1:T(4,128)}, u32[]{:S(2)}) copy-start(s32[32,3]{0,1:T(4,128)} %param.7) | copy-start | bytes 1156
  59.1 39.5 %all-to-all-start = ((s32[32,1,8]{2,1,0:T(1,128)}), s32[32,1,8]{2,1,0:T(1,128)S(1)}, u32[]{:S(2)}, u32[]{:S(2)}) async-start(s32[32,1,8]{2,1,0:T(1,128)} %bitcast.2), calls=%async_computation.1 | async-start | bytes 32768 | tf_op jit(solution)/shard_map/all_to_all | solution.py:42
  98.6 28.1 %all-to-all-start.2 = ((bf16[32,8,1024]{2,1,0:T(8,128)(2,1)}), bf16[32,8,1024]{2,1,0:T(8,128)(2,1)S(1)}, u32[]{:S(2)}, u32[]{:S(2)}) async-start(bf16[32,8,1024]{2,1,0:T(8,128)(2,1)} %get-tuple-element.19), calls=%async_computation.3 | async-start | bytes 1048576 | tf_op jit(solution)/shard_map/all_to_all | solution.py:39
  126.8 14.7 %all-to-all-start.1 = ((s32[3,32,8]{2,0,1:T(4,128)}), s32[3,32,8]{2,0,1:T(4,128)S(1)}, u32[]{:S(2)}, u32[]{:S(2)}) async-start(s32[3,32,8]{2,0,1:T(4,128)} %copy_select_fusion), calls=%async_computation.2 | async-start | bytes 131072 | tf_op jit(solution)/shard_map/all_to_all | solution.py:51
  132.4 51.0 %copy-start.1 = (bf16[256,1024]{1,0:T(8,128)(2,1)S(1)}, bf16[256,1024]{1,0:T(8,128)(2,1)}, u32[]{:S(2)}) copy-start(bf16[256,1024]{1,0:T(8,128)(2,1)} %reduce-scatter.6.cloned.1.call-done) | copy-start | bytes 1572868
  141.5 41.9 %all-to-all-start.3 = ((bf16[3,32,8,1024]{3,2,0,1:T(8,128)(2,1)}), bf16[3,32,8,1024]{3,2,0,1:T(8,128)(2,1)S(1)}, u32[]{:S(2)}, u32[]{:S(2)}) async-start(bf16[3,32,8,1024]{3,2,0,1:T(8,128)(2,1)} %copy.46), calls=%async_computation.4 | async-start | bytes 3145728 | tf_op jit(solution)/shard_map/all_to_all | solution.py:50
  145.5 189.2 %all-gather.5.cloned.1.call-start = ((), (), s32[]{:S(2)}) async-start(), calls=%async_computation.11 | async-start | bytes 4718592 | tf_op jit(solution)/shard_map/all_gather | solution.py:77
  263.2 34.7 %copy-start.3 = (bf16[1,256,1024]{2,1,0:T(8,128)(2,1)S(1)}, bf16[1,256,1024]{2,1,0:T(8,128)(2,1)}, u32[]{:S(2)}) copy-start(bf16[1,256,1024]{2,1,0:T(8,128)(2,1)} %get-tuple-element.18) | copy-start | bytes 1572868
  298.8 1.0 copy-start.2
  300.9 265.1 %reduce-scatter.10.cloned.1.call-start = ((), (), s32[]{:S(2)}) async-start(), calls=%async_computation.13 | async-start | bytes 2162688
  348.1 437.3 %reduce-scatter.8.cloned.1.call-start = ((), (), s32[]{:S(2)}) async-start(), calls=%async_computation.12 | async-start | bytes 2162688 | tf_op jit(solution)/shard_map/reduce_scatter | solution.py:90
Sparse Core Ops, SparseCore 0:
  9.9 36.2 all-gather.2
  57.9 37.2 reduce-scatter.5
  301.0 33.5 all-gather.4
  348.2 217.7 reduce-scatter.9
  570.7 214.6 reduce-scatter.7
where the time goes:
time: 793 us; the launch traced here: 792 us
  waiting for transfers between devices  591 us (75%)
  blocking collectives  107 us (13%)
  matrix products  35.4 us (4%)
  starting transfers between devices  28.3 us (4%)
  between operations  14 us (2%)
  local copies, waits for them, and re-layouts  10.6 us (1%)
    reduce_scatter x1, waiting for transfers between devices, per_device(): lax.psum_scatter(second_local, 'group', scatter_dimension=1, tiled=True)  219 us
    unnamed x6, waiting for transfers between devices  211 us
    all_to_all x1, blocking collectives, per_device(): lax.all_to_all(grad_cand[1:].reshape(listed, owners, piece, width), 'grou...  75.9 us
    all_gather x1, waiting for transfers between devices, per_device(): gathered = lax.all_gather(embeds, 'dp', axis=0, tiled=True)  38.2 us
    all_to_all x1, waiting for transfers between devices, per_device(): lax.all_to_all(outgoing, 'group', split_axis=1, concat_axis=1, tiled=True)  37.7 us
    all_gather x1, waiting for transfers between devices, per_device(): lax.all_gather(grad_proj.astype(jnp.bfloat16), 'dp', axis=0, tiled=True)  33.7 us
    all_to_all x1, blocking collectives, per_device(): lax.all_to_all(summed, 'group', split_axis=0, concat_axis=0, tiled=True)  31 us
    reduce_scatter x1, waiting for transfers between devices, per_device(): lax.psum_scatter(jnp.dot(hidden, w_second, preferred_element_type=jnp.flo...  26.2 us
  transfers between devices with their start and end apart: 9, of which 8 were waited for; matrix products, arithmetic and copies ran while one was open for 2% of the time, Pallas kernels for 0%

commit v1 on v0

v1 whole, which is shorter than its diff:
```python
import jax
import jax.numpy as jnp
from jax import lax
from jax.experimental import pallas as pl
from jax.experimental.pallas import tpu as pltpu
from jax.sharding import Mesh, PartitionSpec as P

EPS = 1e-06
TEMP = 10.0
SHIFT = -5.0
F32, BF16 = jnp.float32, jnp.bfloat16


def gelu_fwd(value):
    return jax.nn.gelu(value, approximate=True)


def gelu_back(pre, grad):
    _, back = jax.vjp(gelu_fwd, pre)
    return back(grad)[0]


def shift(value, axis, step):
    n = lax.axis_size(axis)
    return lax.ppermute(value, axis, [(i, (i + step) % n) for i in range(n)])


def swap_core(value):
    return lax.ppermute(value, "core", [(0, 1), (1, 0)])


def offsets(n):
    out = [0]
    for t in range(1, n // 2):
        out += [-t, t]
    return out + [n // 2]


def slot_of(offset, n):
    table = [0] * n
    for place, t in enumerate(offsets(n)):
        table[t % n] = place
    offset = lax.rem(offset + 2 * n, n)
    return sum(jnp.where(offset == t, table[t], 0) for t in range(1, n))


def ring_gather(block, axis):
    half, rows = lax.axis_size(axis) // 2, block.shape[0] // 2
    out, up, down = [block], block, block
    for _ in range(1, half):
        up, down = shift(up, axis, 1), shift(down, axis, -1)
        out += [up, down]
    return out + [shift(up[:rows], axis, 1), shift(down[rows:], axis, -1)]


def ring_scatter(part, axis, dtype):
    half = lax.axis_size(axis) // 2
    far = part(half)
    rows = far.shape[0] // 2
    up = shift(far[:rows].astype(dtype), axis, 1).astype(F32)
    down = shift(far[rows:].astype(dtype), axis, -1).astype(F32)
    for t in range(half - 1, 0, -1):
        a, b = part(t), part(-t)
        if t == half - 1:
            a = jnp.concatenate([a[:rows] + up, a[rows:]], 0)
            b = jnp.concatenate([b[:rows], b[rows:] + down], 0)
        else:
            a, b = a + up, b + down
        up = shift(a.astype(dtype), axis, 1).astype(F32)
        down = shift(b.astype(dtype), axis, -1).astype(F32)
    return part(0) + up + down


def gather_dp(block):
    own, up, down, far_up, far_down = ring_gather(block, "x")
    near, far = jnp.concatenate([up, down], 0), jnp.concatenate([far_up, far_down], 0)
    pieces = [own, near, far]
    return jnp.concatenate(pieces + [swap_core(p) for p in pieces], 0)


def pair_kernel(n_z, n_y, at_z, at_y, blocks, mult, count, own_ref, own_ids_ref, ids_ref,
                unit_ref, inv_ref, *refs):
    n_a, n_b = n_z + 1, n_y + 1
    pieces_a, pieces_b = refs[:n_a], refs[n_a:n_a + n_b]
    grad_unit_ref, grad_proj_ref, cand_ref, sems = refs[n_a + n_b:]
    width, half = own_ref.shape[1], own_ref.shape[0] // 2

    def start(i, slot):
        for pieces, outer, inner, n_in, part in (
            (pieces_a, at_z[i], at_y[i], n_y, 0),
            (pieces_b, at_y[i], at_z[i], n_z, 1),
        ):
            far = len(pieces) - 2
            source = jnp.where((outer == far) & (inner >= n_in // 2), far + 1, outer)
            row = jnp.where(source == far + 1, inner - n_in // 2, inner) * half
            for k, piece in enumerate(pieces):

                @pl.when(source == k)
                def _():
                    pltpu.make_async_copy(
                        piece.at[pl.ds(pl.multiple_of(row, half), half)],
                        cand_ref.at[slot, pl.ds(part * half, half)],
                        sems.at[slot, part],
                    ).start()

    def wait(slot):
        for part in range(2):
            pltpu.make_async_copy(
                pieces_a[0].at[pl.ds(0, half)],
                cand_ref.at[slot, pl.ds(part * half, half)],
                sems.at[slot, part],
            ).wait()

    def body(i, carry):
        slot = lax.rem(i, 2)

        @pl.when(i + 1 < count[0])
        def _():
            start(i + 1, 1 - slot)

        wait(slot)
        cand = cand_ref[slot]
        logits = lax.dot_general(
            own_ref[...], cand, (((1,), (1,)), ((), ())), preferred_element_type=F32
        ) * (TEMP / width) + SHIFT
        same = own_ids_ref[...] == ids_ref[blocks[i]]
        sign = jnp.where(same, 1.0, -1.0).astype(F32)
        scale = mult[i].astype(F32) * (-TEMP / width)
        weight = (sign * scale / (1.0 + jnp.exp(sign * logits))).astype(BF16)
        grad_unit_ref[...] += jnp.dot(weight, cand, preferred_element_type=F32)
        return carry

    start(0, 0)
    grad_unit_ref[...] = jnp.zeros_like(grad_unit_ref)
    lax.fori_loop(0, count[0], body, 0)
    total, unit = grad_unit_ref[...], unit_ref[...]
    mean = jnp.mean(unit * total, axis=-1, keepdims=True)
    grad_proj_ref[...] = (inv_ref[...] * (total - unit * mean)).astype(BF16)


def pair_grads(lists, own, own_ids, ids, pieces_a, pieces_b, unit, inv):
    rows, width = own.shape
    n_z, n_y = len(pieces_a) - 1, len(pieces_b) - 1
    vmem = pl.BlockSpec(memory_space=pltpu.VMEM)
    smem = pl.BlockSpec(memory_space=pltpu.SMEM)
    return pl.pallas_call(
        lambda *refs: pair_kernel(n_z, n_y, *refs),
        in_specs=[smem] * 5 + [vmem] * 5
        + [pl.BlockSpec(memory_space=pl.ANY)] * (n_z + n_y + 2),
        out_specs=[vmem] * 2,
        out_shape=[
            jax.ShapeDtypeStruct((rows, width), F32),
            jax.ShapeDtypeStruct((rows, width), BF16),
        ],
        scratch_shapes=[
            pltpu.VMEM((2, rows, width), BF16),
            pltpu.SemaphoreType.DMA((2, 2)),
        ],
        compiler_params=pltpu.CompilerParams(vmem_limit_bytes=20 << 20),
    )(*lists, own, own_ids, ids, unit, inv, *pieces_a, *pieces_b)


def partner_lists(neighbors, n_z, n_y):
    owners = n_z * n_y
    z, y = lax.axis_index("z"), lax.axis_index("y")
    me = z * n_y + y
    block = jnp.arange(owners, dtype=jnp.int32)
    listed = neighbors[None, :, :] == block[:, None, None]
    mine = block == me
    out = jnp.sum(jnp.where(mine[None, :, None], listed, False), axis=(1, 2))
    into = jnp.sum(neighbors == me, axis=1)
    mult = (out + into + 2 * mine).astype(jnp.int32)
    used = mult > 0
    place = jnp.sum(used[None, :] & (block[None, :] < block[:, None]), axis=1)
    pick = used[None, :] & (place[None, :] == block[:, None])
    count = jnp.sum(used).astype(jnp.int32)
    pick = jnp.where((block < count)[:, None], pick, used[None, :] & (place[None, :] == count - 1))
    blocks = jnp.sum(jnp.where(pick, block[None, :], 0), axis=1).astype(jnp.int32)
    mult = jnp.sum(jnp.where(pick, mult[None, :], 0), axis=1).astype(jnp.int32)
    at_z = slot_of(blocks // n_y - z, n_z)
    at_y = slot_of(lax.rem(blocks, n_y) - y, n_y)
    lists = (at_z, at_y, blocks, mult)
    return tuple(v.astype(jnp.int32) for v in lists) + (count[None],)


def per_device(embeds, row_ids, neighbors, w_first, w_second):
    n_z, n_y = lax.axis_size("z"), lax.axis_size("y")
    owners = n_z * n_y
    z, y = lax.axis_index("z"), lax.axis_index("y")
    block, width = embeds.shape[0], w_second.shape[1]
    share = w_first.shape[1]
    half = block // 2

    ids = lax.all_gather(row_ids, ("z", "y"), axis=0, tiled=True).reshape(owners, 1, block)
    lists = partner_lists(neighbors, n_z, n_y)

    rows = gather_dp(embeds)
    pre = jnp.dot(rows, w_first, preferred_element_type=F32)
    hidden = gelu_fwd(pre).astype(BF16)
    part = jnp.dot(hidden, w_second, preferred_element_type=F32).astype(BF16)
    n_x = lax.axis_size("x")
    part = part.reshape(2, n_x, block, width)
    pair = part[0].astype(F32) + swap_core(part[1]).astype(F32)
    place = {t: i for i, t in enumerate(offsets(n_x))}
    proj = ring_scatter(lambda t: pair[place[t]], "x", BF16)

    inv = lax.rsqrt(jnp.mean(proj * proj, axis=-1, keepdims=True) + EPS)
    unit = proj * inv
    unit_b = unit.astype(BF16)

    over_y = jnp.concatenate(ring_gather(unit_b[:half], "y"), 0)
    over_z = jnp.concatenate(ring_gather(unit_b[half:], "z"), 0)
    units_a = ring_gather(over_y, "z")
    units_b = ring_gather(over_z, "y")
    grad_unit, grad_proj = pair_grads(
        lists, unit_b, row_ids[:, None], ids, units_a, units_b, unit, inv
    )

    grad_all = gather_dp(grad_proj)
    rows_in = (((0,), (0,)), ((), ()))
    second = lax.dot_general(grad_all, hidden, rows_in, preferred_element_type=F32)
    grad_hidden = lax.dot_general(
        grad_all, w_second, (((1,), (1,)), ((), ())), preferred_element_type=F32
    )
    grad_pre = gelu_back(pre, grad_hidden).astype(BF16)
    first = lax.dot_general(rows, grad_pre, rows_in, preferred_element_type=F32)

    second = lax.psum_scatter(second, "z", scatter_dimension=0, tiled=True)
    second = lax.psum_scatter(second, "y", scatter_dimension=0, tiled=True)

    first = first.reshape(n_z, n_y, -1, share)
    first = ring_scatter(
        lambda t: lax.dynamic_index_in_dim(first, lax.rem(y + t + n_y, n_y), 1, False), "y", F32
    )
    by_z = first
    first = ring_scatter(
        lambda t: lax.dynamic_index_in_dim(by_z, lax.rem(z + t + n_z, n_z), 0, False), "z", F32
    )
    return (first, second.T, grad_unit)


def solution(mesh):
    split = Mesh(mesh.devices.reshape(4, 2, 8, 4), ("x", "core", "z", "y"))
    dp, group = ("x", "core"), ("z", "y")
    in_specs = (P(dp + group, None), P(dp + group), P(dp, None), P(None, dp), P(dp, None))
    out_specs = (P(group, dp), P(dp, group), P(dp + group, None))
    return jax.shard_map(
        per_device, mesh=split, in_specs=in_specs, out_specs=out_specs, check_vma=False
    )
```

time: 793 us -> 410 us (0.52)
  waiting for transfers between devices: 591 us -> 167 us
  starting transfers between devices: 28.3 us -> 96.8 us
  blocking collectives: 107 us -> 51.1 us
  local copies, waits for them, and re-layouts: 10.6 us -> 34.5 us
  matrix products: 35.4 us -> 19.9 us
  other arithmetic: 5.52 us -> 13.7 us
    reduce_scatter x2, waiting for transfers between devices: 246 us -> 15.9 us  [the longest x1 15.9 us: per_device(): second = lax.psum_scatter(second, 'y', scatter_dimension=0, tiled=True)]
    unnamed x6 -> x2, waiting for transfers between devices: 211 us -> 0.03 us
    ppermute x0 -> x55, waiting for transfers between devices: none -> 151 us  [the longest x48 145 us: shift(): return lax.ppermute(value, axis, [(i, (i + step) % n) for i in range(n)])]
    all_to_all x2 -> x0, blocking collectives: 107 us -> none  [the longest x1 75.9 us: per_device(): lax.all_to_all(grad_cand[1:].reshape(listed, owners, piece, width), 'grou...]
    ppermute x0 -> x55, starting transfers between devices: none -> 96.7 us  [the longest x48 96.1 us: shift(): return lax.ppermute(value, axis, [(i, (i + step) % n) for i in range(n)])]
    all_gather x2 -> x0, waiting for transfers between devices: 71.9 us -> none  [the longest x1 38.2 us: per_device(): gathered = lax.all_gather(embeds, 'dp', axis=0, tiled=True)]
    all_to_all x4 -> x0, waiting for transfers between devices: 62.3 us -> none  [the longest x1 37.7 us: per_device(): lax.all_to_all(outgoing, 'group', split_axis=1, concat_axis=1, tiled=True)]
    all_gather x0 -> x1, blocking collectives: none -> 51.1 us  [per_device(): lax.all_gather(row_ids, ('z', 'y'), axis=0, tiled=True)]
  transfers between devices with their start and end apart: 9 -> 57, of which waited for: 8 -> 35; matrix products, arithmetic and copies ran while one was open for 2% -> 10% of each run, Pallas kernels for 0% -> 0%
where the time goes in v1:
time: 410 us; the launch traced here: 406 us
  waiting for transfers between devices  167 us (41%)
  starting transfers between devices  96.8 us (24%)
  blocking collectives  51.1 us (12%)
  local copies, waits for them, and re-layouts  34.5 us (8%)
  matrix products  19.9 us (5%)
  between operations  15.7 us (4%)
  other arithmetic  13.7 us (3%)
  Pallas kernels  6.78 us (2%)
    ppermute x48, waiting for transfers between devices, shift(): return lax.ppermute(value, axis, [(i, (i + step) % n) for i in range(n)])  145 us
    ppermute x48, starting transfers between devices, shift(): return lax.ppermute(value, axis, [(i, (i + step) % n) for i in range(n)])  96.1 us
    all_gather x1, blocking collectives, per_device(): lax.all_gather(row_ids, ('z', 'y'), axis=0, tiled=True)  51.1 us
    unnamed x56, local copies, waits for them, and re-layouts  22.1 us
    reduce_scatter x1, waiting for transfers between devices, per_device(): second = lax.psum_scatter(second, 'y', scatter_dimension=0, tiled=True)  15.9 us
    dot_general x1, matrix products, per_device(): first = lax.dot_general(rows, grad_pre, rows_in, preferred_element_type=F32)  10.9 us
    slice x12, local copies, waits for them, and re-layouts, ring_gather(): return out + [shift(up[:rows], axis, 1), shift(down[rows:], axis, -1)]  9.9 us
  transfers between devices with their start and end apart: 57, of which 35 were waited for; matrix products, arithmetic and copies ran while one was open for 10% of the time, Pallas kernels for 0%

profile of v1, /device:TPU:4, one launch (start us, length us, event | category | flops | bytes accessed | tf_op | source)
XLA Modules:
  0.0 405.5 jit_solution(14691675952188656085)
XLA Ops:
  9.3 11.8 %collective-permute-done = bf16[256,1024]{1,0:T(8,128)(2,1)S(1)} collective-permute-done((bf16[256,1024]{1,0:T(8,128)(2,1)}, bf16[256,1024]{1,0:T(8,128)(2,1)S(1)}, u32[]{:S(2)}, u32[]{:S(2)}) %collective-permute-start) | collective-permute-done | bytes 524320 | tf_op jit(solution)/shard_map/ppermute | solution.py:25
  25.6 5.4 %collective-permute-done.2 = bf16[128,1024]{1,0:T(8,128)(2,1)S(1)} collective-permute-done((bf16[128,1024]{1,0:T(8,128)(2,1)S(1)}, bf16[128,1024]{1,0:T(8,128)(2,1)S(1)}, u32[]{:S(2)}, u32[]{:S(2)}) %collective-permute-start.2) | collective-permute-done | bytes 262176 | tf_op jit(solution)/shard_map/ppermute | solution.py:25
  44.4 4.0 collective-permute-done.7
  52.1 6.3 %collective-permute-done.10 = bf16[128,1024]{1,0:T(8,128)(2,1)S(1)} collective-permute-done((bf16[128,1024]{1,0:T(8,128)(2,1)S(1)}, bf16[128,1024]{1,0:T(8,128)(2,1)S(1)}, u32[]{:S(2)}, u32[]{:S(2)}) %collective-permute-start.10) | collective-permute-done | bytes 262176 | tf_op jit(solution)/shard_map/ppermute | solution.py:25
  61.6 10.7 %collective-permute-done.9 = bf16[256,1024]{1,0:T(8,128)(2,1)S(1)} collective-permute-done((bf16[256,1024]{1,0:T(8,128)(2,1)S(1)}, bf16[256,1024]{1,0:T(8,128)(2,1)S(1)}, u32[]{:S(2)}, u32[]{:S(2)}) %collective-permute-start.9) | collective-permute-done | bytes 524320 | tf_op jit(solution)/shard_map/ppermute | solution.py:25
  81.9 3.9 collective-permute-start.25
  109.6 3.8 collective-permute-start.31
  114.8 14.1 %collective-permute-done.30 = bf16[64,1024]{1,0:T(8,128)(2,1)S(1)} collective-permute-done((bf16[64,1024]{1,0:T(8,128)(2,1)S(1)}, bf16[64,1024]{1,0:T(8,128)(2,1)S(1)}, u32[]{:S(2)}, u32[]{:S(2)}) %collective-permute-start.30) | collective-permute-done | bytes 131104 | tf_op jit(solution)/shard_map/ppermute | solution.py:25
  138.8 17.9 %collective-permute-done.18.refs_13_ = bf16[512,1024]{1,0:T(8,128)(2,1)} collective-permute-done((bf16[512,1024]{1,0:T(8,128)(2,1)S(1)}, bf16[512,1024]{1,0:T(8,128)(2,1)}, u32[]{:S(2)}, u32[]{:S(2)}) %collective-permute-start.18) | collective-permute-done | bytes 1048608 | tf_op jit(solution)/shard_map/ppermute | solution.py:25
  157.2 3.7 collective-permute-start.21
  161.2 12.9 %collective-permute-done.32.refs_20_ = bf16[1024,1024]{1,0:T(8,128)(2,1)} collective-permute-done((bf16[1024,1024]{1,0:T(8,128)(2,1)}, bf16[1024,1024]{1,0:T(8,128)(2,1)}, u32[]{:S(2)}, u32[]{:S(2)}) %collective-permute-start.32) | collective-permute-done | bytes 2097184 | tf_op jit(solution)/shard_map/ppermute | solution.py:25
  183.2 51.1 %all-gather.refs_7_ = s32[32,1,256]{2,1,0:T(1,128)S(1)} all-gather(s32[1,1,256]{2,1,0:T(1,128)S(1)} %bitcast.117), channel_id=1, replica_groups=mesh['x'=4,'core'=2,'z'=8,'y'=4] {'z','y'}, dimensions={0}, use_global_device_ids=true | all-gather | bytes 33792 | tf_op jit(solution)/shard_map/all_gather | solution.py:194
  242.4 4.4 %collective-permute-done.22.refs_17_ = bf16[256,1024]{1,0:T(8,128)(2,1)S(1)} collective-permute-done((bf16[256,1024]{1,0:T(8,128)(2,1)}, bf16[256,1024]{1,0:T(8,128)(2,1)S(1)}, u32[]{:S(2)}, u32[]{:S(2)}) %collective-permute-start.22) | collective-permute-done | bytes 524320 | tf_op jit(solution)/shard_map/ppermute | solution.py:25
  253.4 6.8 %shard_map.76 = (f32[256,1024]{1,0:T(8,128)}, bf16[256,1024]{1,0:T(8,128)(2,1)S(1)}) custom-call(s32[32]{0:T(128)S(1)} %get-tuple-element.42.refs_0_, s32[32]{0:T(128)S(1)} %get-tuple-element.41.refs_1_, s32[32]{0:T(128)S(1)} %get-tuple-element.8.refs_2_, s32[32]{0:T(128)S(1)} %get-tuple-element.7.refs_3_, s32[1]{0:T(128)} %bitcast.refs_4_, ...), custom_call_target="tpu_custom_call" | custom-call | tf_op jit(solution)/shard_map/pallas_call | solution.py:146
  262.9 6.8 %collective-permute-done.36 = bf16[256,1024]{1,0:T(8,128)(2,1)S(1)} collective-permute-done((bf16[256,1024]{1,0:T(8,128)(2,1)S(1)}, bf16[256,1024]{1,0:T(8,128)(2,1)S(1)}, u32[]{:S(2)}, u32[]{:S(2)}) %collective-permute-start.36) | collective-permute-done | bytes 524320 | tf_op jit(solution)/shard_map/ppermute | solution.py:25
  277.8 4.9 %collective-permute-done.38 = bf16[128,1024]{1,0:T(8,128)(2,1)S(1)} collective-permute-done((bf16[128,1024]{1,0:T(8,128)(2,1)}, bf16[128,1024]{1,0:T(8,128)(2,1)S(1)}, u32[]{:S(2)}, u32[]{:S(2)}) %collective-permute-start.38) | collective-permute-done | bytes 262176 | tf_op jit(solution)/shard_map/ppermute | solution.py:25
  290.3 3.8 fusion.42
  294.2 10.9 %fusion.7 = f32[1024,512]{1,0:T(8,128)S(1)} fusion(bf16[2048,1024]{1,0:T(8,128)(2,1)} %copy-done.9, f32[2048,512]{1,0:T(8,128)} %copy-done.14, bf16[2048,1024]{1,0:T(8,128)(2,1)} %copy-done.10, bf16[512,1024]{1,0:T(8,128)(2,1)S(1)} %copy-done), kind=kOutput, calls=%fused_computation.12 | convolution fusion | flops 4315938816 | bytes 15728640 | tf_op jit(solution)/shard_map/dot_general | solution.py:226
  306.9 13.4 %collective-permute-start.45 = (f32[4,32,512]{2,1,0:T(8,128)S(1)}, f32[4,32,512]{2,1,0:T(8,128)S(1)}, u32[]{:S(2)}, u32[]{:S(2)}) collective-permute-start(f32[4,32,512]{2,1,0:T(8,128)S(1)} %get-tuple-element.23), channel_id=1, source_target_pairs={{0,3},{1,0},{2,1},{3,2},{4,7},{5,4},{6,5},{7,6},{8,11},{9,8},{10,9... | collective-permute-start | bytes 786440 | tf_op jit(solution)/shard_map/ppermute | solution.py:25
  320.3 6.5 %collective-permute-done.43 = f32[4,32,512]{2,1,0:T(8,128)S(1)} collective-permute-done((f32[4,32,512]{2,1,0:T(8,128)S(1)}, f32[4,32,512]{2,1,0:T(8,128)S(1)}, u32[]{:S(2)}, u32[]{:S(2)}) %collective-permute-start.43) | collective-permute-done | bytes 262176 | tf_op jit(solution)/shard_map/ppermute | solution.py:25
  331.8 10.9 %collective-permute-done.44 = f32[8,32,512]{2,1,0:T(8,128)} collective-permute-done((f32[8,32,512]{2,1,0:T(8,128)}, f32[8,32,512]{2,1,0:T(8,128)}, u32[]{:S(2)}, u32[]{:S(2)}) %collective-permute-start.44) | collective-permute-done | bytes 524320 | tf_op jit(solution)/shard_map/ppermute | solution.py:25
  346.2 4.9 %collective-permute-start.51 = (f32[16,512]{1,0:T(8,128)S(1)}, f32[16,512]{1,0:T(8,128)S(1)}, u32[]{:S(2)}, u32[]{:S(2)}) collective-permute-start(f32[16,512]{1,0:T(8,128)S(1)} %get-tuple-element.35), channel_id=1, source_target_pairs={{0,28},{4,0},{8,4},{12,8},{16,12},{20,16},{24,20},{28,24},{1,29},{... | collective-permute-start | bytes 98312 | tf_op jit(solution)/shard_map/ppermute | solution.py:25
  353.7 7.5 %collective-permute-start.48 = (f32[32,512]{1,0:T(8,128)S(1)}, f32[32,512]{1,0:T(8,128)S(1)}, u32[]{:S(2)}, u32[]{:S(2)}) collective-permute-start(f32[32,512]{1,0:T(8,128)S(1)} %pad_maximum_fusion.8), channel_id=1, source_target_pairs={{0,4},{4,8},{8,12},{12,16},{16,20},{20,24},{24,28},{28,0},{1,5},{5... | collective-permute-start | bytes 196616 | tf_op jit(solution)/shard_map/ppermute | solution.py:25
  382.3 15.9 %reduce-scatter.5.cloned.1.call-done = f32[32,512]{1,0:T(8,128)} async-done(((f32[128,512]{1,0:T(8,128)}), f32[32,512]{1,0:T(8,128)}) %reduce-scatter.5.cloned.1.call-update) | async-done | bytes 65552 | tf_op jit(solution)/shard_map/reduce_scatter | solution.py:229
  (208 shorter events, 147.4 us)
Async XLA Ops:
  7.2 364.2 %reduce-scatter.3.cloned.1.call-start = ((), (), s32[]{:S(2)}) async-start(), calls=%async_computation.2 | async-start | bytes 2359296 | tf_op jit(solution)/shard_map/reduce_scatter | solution.py:228
  7.2 14.0 %collective-permute-start = (bf16[256,1024]{1,0:T(8,128)(2,1)}, bf16[256,1024]{1,0:T(8,128)(2,1)S(1)}, u32[]{:S(2)}, u32[]{:S(2)}) collective-permute-start(bf16[256,1024]{1,0:T(8,128)(2,1)} %param.5), channel_id=1, source_target_pairs={{0,64},{64,128},{128,192},{192,0},{1,65},{65,129},{129,193},{193,1... | collective-permute-start | bytes 1572872 | tf_op jit(solution)/shard_map/ppermute | solution.py:25
  8.5 13.6 %collective-permute-start.1 = (bf16[256,1024]{1,0:T(8,128)(2,1)}, bf16[256,1024]{1,0:T(8,128)(2,1)S(1)}, u32[]{:S(2)}, u32[]{:S(2)}) collective-permute-start(bf16[256,1024]{1,0:T(8,128)(2,1)} %param.5), channel_id=1, source_target_pairs={{0,192},{64,0},{128,64},{192,128},{1,193},{65,1},{129,65},{193,129... | collective-permute-start | bytes 1572872 | tf_op jit(solution)/shard_map/ppermute | solution.py:25
  58.8 13.5 %collective-permute-start.9 = (bf16[256,1024]{1,0:T(8,128)(2,1)S(1)}, bf16[256,1024]{1,0:T(8,128)(2,1)S(1)}, u32[]{:S(2)}, u32[]{:S(2)}) collective-permute-start(bf16[256,1024]{1,0:T(8,128)(2,1)S(1)} %pad_maximum_fusion.3), channel_id=1, source_target_pairs={{0,64},{64,128},{128,192},{192,0},{1,65},{65,129},{129,193},{193,1... | collective-permute-start | bytes 1572872 | tf_op jit(solution)/shard_map/ppermute | solution.py:25
  61.5 13.8 %collective-permute-start.11 = (bf16[256,1024]{1,0:T(8,128)(2,1)S(1)}, bf16[256,1024]{1,0:T(8,128)(2,1)S(1)}, u32[]{:S(2)}, u32[]{:S(2)}) collective-permute-start(bf16[256,1024]{1,0:T(8,128)(2,1)S(1)} %pad_maximum_fusion.4), channel_id=1, source_target_pairs={{0,192},{64,0},{128,64},{192,128},{1,193},{65,1},{129,65},{193,129... | collective-permute-start | bytes 1572872 | tf_op jit(solution)/shard_map/ppermute | solution.py:25
  86.3 16.4 %collective-permute-start.15 = (bf16[64,1024]{1,0:T(8,128)(2,1)S(1)}, bf16[64,1024]{1,0:T(8,128)(2,1)S(1)}, u32[]{:S(2)}, u32[]{:S(2)}) collective-permute-start(bf16[64,1024]{1,0:T(8,128)(2,1)S(1)} %slice.234), channel_id=1, source_target_pairs={{0,3},{1,0},{2,1},{3,2},{4,7},{5,4},{6,5},{7,6},{8,11},{9,8},{10,9... | collective-permute-start | bytes 393224 | tf_op jit(solution)/shard_map/ppermute | solution.py:25
  102.8 30.7 %collective-permute-start.16 = (bf16[512,1024]{1,0:T(8,128)(2,1)S(1)}, bf16[512,1024]{1,0:T(8,128)(2,1)S(1)}, u32[]{:S(2)}, u32[]{:S(2)}) collective-permute-start(bf16[512,1024]{1,0:T(8,128)(2,1)S(1)} %constant_dynamic-update-slice_fusion.8.refs_10_), channel_id=1, source_target_pairs={{0,4},{4,8},{8,12},{12,16},{16,20},{20,24},{24,28},{28,0},{1,5},{5... | collective-permute-start | bytes 3145736 | tf_op jit(solution)/shard_map/ppermute | solution.py:25
  102.9 31.6 %collective-permute-start.17 = (bf16[512,1024]{1,0:T(8,128)(2,1)S(1)}, bf16[512,1024]{1,0:T(8,128)(2,1)S(1)}, u32[]{:S(2)}, u32[]{:S(2)}) collective-permute-start(bf16[512,1024]{1,0:T(8,128)(2,1)S(1)} %constant_dynamic-update-slice_fusion.8.refs_10_), channel_id=1, source_target_pairs={{0,28},{4,0},{8,4},{12,8},{16,12},{20,16},{24,20},{28,24},{1,29},{... | collective-permute-start | bytes 3145736 | tf_op jit(solution)/shard_map/ppermute | solution.py:25
  109.1 19.9 %collective-permute-start.30 = (bf16[64,1024]{1,0:T(8,128)(2,1)S(1)}, bf16[64,1024]{1,0:T(8,128)(2,1)S(1)}, u32[]{:S(2)}, u32[]{:S(2)}) collective-permute-start(bf16[64,1024]{1,0:T(8,128)(2,1)S(1)} %slice.238), channel_id=1, source_target_pairs={{0,4},{4,8},{8,12},{12,16},{16,20},{20,24},{24,28},{28,0},{1,5},{5... | collective-permute-start | bytes 393224 | tf_op jit(solution)/shard_map/ppermute | solution.py:25
  109.6 20.0 %collective-permute-start.31 = (bf16[64,1024]{1,0:T(8,128)(2,1)S(1)}, bf16[64,1024]{1,0:T(8,128)(2,1)S(1)}, u32[]{:S(2)}, u32[]{:S(2)}) collective-permute-start(bf16[64,1024]{1,0:T(8,128)(2,1)S(1)} %slice.239), channel_id=1, source_target_pairs={{0,28},{4,0},{8,4},{12,8},{16,12},{20,16},{24,20},{28,24},{1,29},{... | collective-permute-start | bytes 393224 | tf_op jit(solution)/shard_map/ppermute | solution.py:25
  130.3 43.8 %collective-permute-start.32 = (bf16[1024,1024]{1,0:T(8,128)(2,1)}, bf16[1024,1024]{1,0:T(8,128)(2,1)}, u32[]{:S(2)}, u32[]{:S(2)}) collective-permute-start(bf16[1024,1024]{1,0:T(8,128)(2,1)} %constant_dynamic-update-slice_fusion.13.refs_19_), channel_id=1, source_target_pairs={{0,1},{1,2},{2,3},{3,0},{4,5},{5,6},{6,7},{7,4},{8,9},{9,10},{10,1... | collective-permute-start | bytes 6291464 | tf_op jit(solution)/shard_map/ppermute | solution.py:25
  130.4 45.9 %collective-permute-start.33 = (bf16[1024,1024]{1,0:T(8,128)(2,1)}, bf16[1024,1024]{1,0:T(8,128)(2,1)}, u32[]{:S(2)}, u32[]{:S(2)}) collective-permute-start(bf16[1024,1024]{1,0:T(8,128)(2,1)} %constant_dynamic-update-slice_fusion.13.refs_19_), channel_id=1, source_target_pairs={{0,3},{1,0},{2,1},{3,2},{4,7},{5,4},{6,5},{7,6},{8,11},{9,8},{10,9... | collective-permute-start | bytes 6291464 | tf_op jit(solution)/shard_map/ppermute | solution.py:25
  133.5 23.1 %collective-permute-start.18 = (bf16[512,1024]{1,0:T(8,128)(2,1)S(1)}, bf16[512,1024]{1,0:T(8,128)(2,1)}, u32[]{:S(2)}, u32[]{:S(2)}) collective-permute-start(bf16[512,1024]{1,0:T(8,128)(2,1)S(1)} %collective-permute-done.16.refs_11_), channel_id=1, source_target_pairs={{0,4},{4,8},{8,12},{12,16},{16,20},{20,24},{24,28},{28,0},{1,5},{5... | collective-permute-start | bytes 3145736 | tf_op jit(solution)/shard_map/ppermute | solution.py:25
  134.5 22.6 %collective-permute-start.19 = (bf16[512,1024]{1,0:T(8,128)(2,1)S(1)}, bf16[512,1024]{1,0:T(8,128)(2,1)}, u32[]{:S(2)}, u32[]{:S(2)}) collective-permute-start(bf16[512,1024]{1,0:T(8,128)(2,1)S(1)} %collective-permute-done.17.refs_12_), channel_id=1, source_target_pairs={{0,28},{4,0},{8,4},{12,8},{16,12},{20,16},{24,20},{28,24},{1,29},{... | collective-permute-start | bytes 3145736 | tf_op jit(solution)/shard_map/ppermute | solution.py:25
  156.6 77.8 %collective-permute-start.20 = (bf16[512,1024]{1,0:T(8,128)(2,1)}, bf16[512,1024]{1,0:T(8,128)(2,1)}, u32[]{:S(2)}, u32[]{:S(2)}) collective-permute-start(bf16[512,1024]{1,0:T(8,128)(2,1)} %collective-permute-done.18.refs_13_), channel_id=1, source_target_pairs={{0,4},{4,8},{8,12},{12,16},{16,20},{20,24},{24,28},{28,0},{1,5},{5... | collective-permute-start | bytes 3145736 | tf_op jit(solution)/shard_map/ppermute | solution.py:25
  157.2 81.1 %collective-permute-start.21 = (bf16[512,1024]{1,0:T(8,128)(2,1)}, bf16[512,1024]{1,0:T(8,128)(2,1)}, u32[]{:S(2)}, u32[]{:S(2)}) collective-permute-start(bf16[512,1024]{1,0:T(8,128)(2,1)} %collective-permute-done.19.refs_14_), channel_id=1, source_target_pairs={{0,28},{4,0},{8,4},{12,8},{16,12},{20,16},{24,20},{28,24},{1,29},{... | collective-permute-start | bytes 3145736 | tf_op jit(solution)/shard_map/ppermute | solution.py:25
  176.3 66.1 %collective-permute-start.34 = (bf16[512,1024]{1,0:T(8,128)(2,1)}, bf16[512,1024]{1,0:T(8,128)(2,1)}, u32[]{:S(2)}, u32[]{:S(2)}) collective-permute-start(bf16[512,1024]{1,0:T(8,128)(2,1)} %slice.240), channel_id=1, source_target_pairs={{0,1},{1,2},{2,3},{3,0},{4,5},{5,6},{6,7},{7,4},{8,9},{9,10},{10,1... | collective-permute-start | bytes 3145736 | tf_op jit(solution)/shard_map/ppermute | solution.py:25
  178.7 63.7 %collective-permute-start.35 = (bf16[512,1024]{1,0:T(8,128)(2,1)}, bf16[512,1024]{1,0:T(8,128)(2,1)}, u32[]{:S(2)}, u32[]{:S(2)}) collective-permute-start(bf16[512,1024]{1,0:T(8,128)(2,1)} %slice.241), channel_id=1, source_target_pairs={{0,3},{1,0},{2,1},{3,2},{4,7},{5,4},{6,5},{7,6},{8,11},{9,8},{10,9... | collective-permute-start | bytes 3145736 | tf_op jit(solution)/shard_map/ppermute | solution.py:25
  273.1 14.3 %collective-permute-start.41 = (bf16[512,1024]{1,0:T(8,128)(2,1)}, bf16[512,1024]{1,0:T(8,128)(2,1)S(1)}, u32[]{:S(2)}, u32[]{:S(2)}) collective-permute-start(bf16[512,1024]{1,0:T(8,128)(2,1)} %pad_maximum_fusion.1), channel_id=1, source_target_pairs={{0,32},{32,0},{1,33},{33,1},{2,34},{34,2},{3,35},{35,3},{4,36},{36... | collective-permute-start | bytes 3145736 | tf_op jit(solution)/shard_map/ppermute | solution.py:29
  294.1 104.1 %reduce-scatter.5.cloned.1.call-start = ((), (), s32[]{:S(2)}) async-start(), calls=%async_computation.3 | async-start | bytes 327680 | tf_op jit(solution)/shard_map/reduce_scatter | solution.py:229
  305.2 21.6 %collective-permute-start.43 = (f32[4,32,512]{2,1,0:T(8,128)S(1)}, f32[4,32,512]{2,1,0:T(8,128)S(1)}, u32[]{:S(2)}, u32[]{:S(2)}) collective-permute-start(f32[4,32,512]{2,1,0:T(8,128)S(1)} %get-tuple-element.21), channel_id=1, source_target_pairs={{0,1},{1,2},{2,3},{3,0},{4,5},{5,6},{6,7},{7,4},{8,9},{9,10},{10,1... | collective-permute-start | bytes 786440 | tf_op jit(solution)/shard_map/ppermute | solution.py:25
  306.9 19.9 %collective-permute-start.45 = (f32[4,32,512]{2,1,0:T(8,128)S(1)}, f32[4,32,512]{2,1,0:T(8,128)S(1)}, u32[]{:S(2)}, u32[]{:S(2)}) collective-permute-start(f32[4,32,512]{2,1,0:T(8,128)S(1)} %get-tuple-element.23), channel_id=1, source_target_pairs={{0,3},{1,0},{2,1},{3,2},{4,7},{5,4},{6,5},{7,6},{8,11},{9,8},{10,9... | collective-permute-start | bytes 786440 | tf_op jit(solution)/shard_map/ppermute | solution.py:25
  327.7 15.0 %collective-permute-start.44 = (f32[8,32,512]{2,1,0:T(8,128)}, f32[8,32,512]{2,1,0:T(8,128)}, u32[]{:S(2)}, u32[]{:S(2)}) collective-permute-start(f32[8,32,512]{2,1,0:T(8,128)} %pad_maximum_fusion.6), channel_id=1, source_target_pairs={{0,1},{1,2},{2,3},{3,0},{4,5},{5,6},{6,7},{7,4},{8,9},{9,10},{10,1... | collective-permute-start | bytes 1572872 | tf_op jit(solution)/shard_map/ppermute | solution.py:25
  329.7 13.2 %collective-permute-start.46 = (f32[8,32,512]{2,1,0:T(8,128)}, f32[8,32,512]{2,1,0:T(8,128)}, u32[]{:S(2)}, u32[]{:S(2)}) collective-permute-start(f32[8,32,512]{2,1,0:T(8,128)} %pad_maximum_fusion.7), channel_id=1, source_target_pairs={{0,3},{1,0},{2,1},{3,2},{4,7},{5,4},{6,5},{7,6},{8,11},{9,8},{10,9... | collective-permute-start | bytes 1572872 | tf_op jit(solution)/shard_map/ppermute | solution.py:25
  (49 other events, 506.3 us)
Sparse Core Ops, SparseCore 0:
  294.2 62.6 reduce-scatter.2
  371.6 26.6 reduce-scatter.4
